TPU v7x, 32 devices: a whole 2x2x4 slice. The times are simulated.
32 devices in a mesh: dp: 8 (over z, x), tensor: 4 (over y, core).
Axes of the slice: x: 2, y: 2, z: 4, core: 2. Of those that a mesh axis runs over, the one named last changes fastest.
Arguments:
- inputs: bfloat16 [2048, 2048], P('dp'), may hold values from -6 to 6
- document: int32 [2048], P('dp'), may hold values from 0 to 8, as said below
- query_weight: bfloat16 [2048, 2048], P(None, 'tensor'), may hold values from -0.125 to 0.125
- key_weight: bfloat16 [2048, 2048], P(None, 'tensor'), may hold values from -0.125 to 0.125
- value_weight: bfloat16 [2048, 3456], P(None, 'tensor'), may hold values from -0.125 to 0.125
- gate_weight: bfloat16 [2048, 3456], P(None, 'tensor'), may hold values from -0.125 to 0.125
- out_weight: bfloat16 [3456, 2048], P('tensor'), may hold values from -0.109375 to 0.109375
- inner_weight: bfloat16 [2048, 3456], P(None, 'tensor'), may hold values from -0.125 to 0.125
- linear_weight: bfloat16 [2048, 3456], P(None, 'tensor'), may hold values from -0.125 to 0.125
- down_weight: bfloat16 [3456, 2048], P('tensor'), may hold values from -0.109375 to 0.109375
- first_gain: float32 [2048], replicated, may hold values from 0.5 to 1.5
- first_bias: float32 [2048], replicated, may hold values from -3 to 3
- head_gain: float32 [3456], P('tensor'), may hold values from 0.5 to 1.5
- second_gain: float32 [2048], replicated, may hold values from 0.5 to 1.5
- second_bias: float32 [2048], replicated, may hold values from -3 to 3
- cotangent: bfloat16 [2048, 2048], P('dp'), may hold values from -8 to 8
Outputs:
- outputs: float32 [2048, 2048], P('dp')
- grad_inputs: float32 [2048, 2048], P('dp')
- grad_query: float32 [2048, 2048], P('dp', 'tensor')
- grad_key: float32 [2048, 2048], P('dp', 'tensor')
- grad_value: float32 [2048, 3456], P('dp', 'tensor')
- grad_gate: float32 [2048, 3456], P('dp', 'tensor')
- grad_out: float32 [3456, 2048], P('tensor', 'dp')
- grad_inner: float32 [2048, 3456], P('dp', 'tensor')
- grad_linear: float32 [2048, 3456], P('dp', 'tensor')
- grad_down: float32 [3456, 2048], P('tensor', 'dp')
- grad_first_gain: float32 [2048], replicated
- grad_first_bias: float32 [2048], replicated
- grad_head_gain: float32 [3456], P('tensor')
- grad_second_gain: float32 [2048], replicated
- grad_second_bias: float32 [2048], replicated
Inputs may be any that keep to these rules, and one draw needn't show every extreme that they name: `document`: within each dp block of 256 slots the sequence numbers never fall; the live slots come first and hold numbers below 8, the last live one 8 - 1; the other slots hold 8. One block is all live and another has exactly 128 live slots.
All inputs are finite; a program needn't handle non-finite values.
Results may differ from a plain program's by a relative error of at most 0.015.
Values sent between devices are 32-bit elements; how exact they have to be, the bound alone decides.
No kernel may reach another device: no remote copies, remote signals or barrier semaphores. Data moves between devices by JAX's collectives and lax.ppermute only.
A program may use at most 192 MiB of HBM per device.

v0:
```python
import functools
from types import SimpleNamespace

import jax
import jax.numpy as jnp
from jax import lax
from jax.experimental import pallas as pl
from jax.experimental.pallas import tpu as pltpu
from jax.sharding import PartitionSpec as P

KD = 256
VD = 432
DOCS_DEV = 8
SIDE = 1
NEXT = 2
FAR = 4
BITS = 8

EPS = 1e-05
HEAD_EPS = 0.25
SCALE = KD ** (-0.5)

F32 = jnp.float32
BF16 = jnp.bfloat16
AXES = ("dp", "tensor")


def dot(a, b, ca, cb):
    return lax.dot_general(a, b, (((ca,), (cb,)), ((), ())), preferred_element_type=F32)


def nn(a, b):
    return dot(a, b, 1, 0)


def nt(a, b):
    return dot(a, b, 1, 1)


def tn(a, b):
    return dot(a, b, 0, 0)


def standard(value, epsilon, axis):
    center = value - jnp.mean(value, axis, keepdims=True)
    inverse = lax.rsqrt(jnp.mean(center * center, axis, keepdims=True) + epsilon)
    return center * inverse, inverse


def norm_back(upstream, unit, inverse, gain, axis):
    scaled = upstream * gain
    return inverse * (
        scaled
        - jnp.mean(scaled, axis, keepdims=True)
        - unit * jnp.mean(scaled * unit, axis, keepdims=True)
    )


class Call:
    def __init__(self, blocks, rows=None):
        self.blocks, self.rows = blocks, rows
        self.keys, self.arrays, self.specs = [], [], []
        self.out_keys, self.outs, self.out_specs = [], [], []
        self.temp_keys, self.temps = [], []

    def add(self, key, array, spec):
        self.keys.append(key)
        self.arrays.append(array)
        self.specs.append(spec)

    def spec(self, shape, **mode):
        if self.rows and shape[0] == self.rows:
            return pl.BlockSpec((self.rows // self.blocks, shape[1]), lambda b: (b, 0))
        return pl.BlockSpec(shape, zeros(len(shape)), **mode)

    def whole(self, **arrays):
        for key, array in arrays.items():
            self.add(key, array, self.spec(array.shape, pipeline_mode=pl.Buffered(1)))

    def scalars(self, **arrays):
        for key, array in arrays.items():
            self.add(key, array, pl.BlockSpec(memory_space=pltpu.SMEM))

    def cut(self, **arrays):
        for key, array in arrays.items():
            self.add(key, array, leading(array.shape[1:]))

    def pieces(self, **groups):
        for key, group in groups.items():
            for block, runs in enumerate(group):
                for run, parts in enumerate(runs):
                    for part in parts:
                        spec = self.spec(part.shape, pipeline_mode=pl.Buffered(1))
                        self.add((key, block, run), part, spec)

    def after(self, *arrays):
        for array in arrays:
            self.add(None, array, pl.BlockSpec(memory_space=pl.ANY))

    def result(self, **forms):
        for key, (shape, dtype) in forms.items():
            self.out_keys.append(key)
            self.outs.append(jax.ShapeDtypeStruct(shape, dtype))
            self.out_specs.append(self.spec(shape))

    def results(self, **forms):
        for key, (shape, dtype) in forms.items():
            self.out_keys.append(key)
            self.outs.append(jax.ShapeDtypeStruct((self.blocks,) + shape, dtype))
            self.out_specs.append(leading(shape))

    def temp(self, **forms):
        for key, (shape, dtype) in forms.items():
            self.temp_keys.append(key)
            self.temps.append(pltpu.VMEM(shape, dtype))

    def run(self, name, body):
        keys = self.keys + self.out_keys + self.temp_keys

        def kernel(*refs):
            r = SimpleNamespace()
            for key, ref in zip(keys, refs):
                if isinstance(key, tuple):
                    runs = r.__dict__.setdefault(key[0], {}).setdefault(key[1], {})
                    runs.setdefault(key[2], []).append(ref)
                elif key is not None:
                    setattr(r, key, ref)
            body(r)

        got = pl.pallas_call(
            kernel,
            grid=(self.blocks,),
            in_specs=self.specs,
            out_specs=self.out_specs,
            out_shape=self.outs,
            scratch_shapes=self.temps,
            cost_estimate=LIGHT,
            name=name,
        )(*self.arrays)
        return SimpleNamespace(**dict(zip(self.out_keys, got)))


LIGHT = pl.CostEstimate(flops=1, transcendentals=0, bytes_accessed=1)


def zeros(n):
    return lambda *g: (0,) * n


def leading(shape):
    rest = (0,) * len(shape)
    return pl.BlockSpec((None,) + shape, lambda b: (b,) + rest)


STEP = 32


def by_rows(rows, step, run):
    @pl.loop(0, rows // step)
    def _(i):
        run(pl.ds(pl.multiple_of(i * step, step), step))


def place_pieces(r, target, group, width):
    core = r.info[0]
    row = r.info[1]

    def put(runs):
        first = 0
        for parts in runs.values():
            size = width // len(parts)
            if len(parts) == 4:
                far = (1 - core) * 2
                at = [core * 2 + row, core * 2 + 1 - row, far + row, far + 1 - row]
            else:
                at = [core, 1 - core]
            cuts = [pl.ds(pl.multiple_of(a * size, size), size) for a in at]

            def move(here, start=first):
                for part, cut in zip(parts, cuts):
                    there = pl.ds(pl.multiple_of(start + here.start, STEP), STEP)
                    target[there, cut] = part[here, :]

            by_rows(parts[0].shape[0], STEP, move)
            first += parts[0].shape[0]

    if len(group) == 1:
        put(group[0])
    else:
        for block, runs in group.items():
            pl.when(pl.program_id(0) == block)(functools.partial(put, runs))


def downwards(r):
    across = r.document[...].astype(F32)
    rows = across.shape[1]
    return jnp.broadcast_to(across, (rows, rows)).T


def decays(r, heads):
    down = downwards(r)
    rows = down.shape[0]
    n = lax.broadcasted_iota(jnp.int32, (rows, rows), 0)
    m = lax.broadcasted_iota(jnp.int32, (rows, rows), 1)
    allowed = (n >= m) & (down == r.document[...].astype(F32))
    spread = jnp.where(allowed, (n - m).astype(F32), 0.0)
    return [jnp.where(allowed, jnp.exp(spread * r.rates[h]), 0.0) for h in range(heads)]


def half_columns(r, width):
    size = width // 2
    return [pl.ds(pl.multiple_of(a * size, size), size) for a in (r.info[0], 1 - r.info[0])]


def attend(own, name, source, document, shared, weights, heads, after=()):
    query_w, key_w, value_wt, gate_wt, out_w = weights
    blocks, unused, rows = document.shape
    width = query_w.shape[0]
    features = value_wt.shape[0]
    c = Call(blocks)
    c.scalars(info=shared.info, rates=shared.rates)
    c.whole(gain=shared.first_gain, bias=shared.first_bias, head_gain=shared.head_gain)
    c.cut(document=document)
    c.whole(qw=query_w, kw=key_w, vw=value_wt, gw=gate_wt)
    c.after(*after)
    if own:
        c.whole(x=source, ow=out_w)
        part = ((rows, width // 2), F32)
        c.result(near=part, away=part)
    else:
        c.pieces(x=source)
        c.temp(x_rows=((rows, width), F32))
    wide = ((rows, heads * KD), BF16)
    tall = ((features, rows), BF16)
    tall_f = ((features, rows), F32)
    c.results(
        normed=((rows, width), BF16),
        q=wide,
        k=wide,
        v=tall,
        s=((heads, rows, rows), BF16),
        g=tall_f,
        hat=tall_f,
        inv=((heads, 1, rows), F32),
        gated=tall,
    )

    def body(r):
        if own:
            x = r.x[...].astype(F32)
        else:
            place_pieces(r, r.x_rows, r.x, width)
            x = r.x_rows[...]
        hat, unused = standard(x, EPS, 1)
        normed = (hat * r.gain[...] + r.bias[...]).astype(BF16)
        r.normed[...] = normed
        r.q[...] = nn(normed, r.qw[...]).astype(BF16)
        r.k[...] = (nn(normed, r.kw[...]) * SCALE).astype(BF16)
        r.v[...] = nt(r.vw[...], normed).astype(BF16)
        r.g[...] = nt(r.gw[...], normed)
        decay = decays(r, heads)
        for h in range(heads):
            kd = pl.ds(h * KD, KD)
            vd = pl.ds(h * VD, VD)
            score = (nt(r.q[:, kd], r.k[:, kd]) * decay[h]).astype(BF16)
            r.s[h] = score
            head_hat, head_inv = standard(nt(r.v[vd, :], score), HEAD_EPS, 0)
            r.hat[vd, :] = head_hat
            r.inv[h] = head_inv
            gates = r.g[vd, :]
            swish = gates * jax.nn.sigmoid(gates)
            r.gated[vd, :] = (swish * (head_hat * r.head_gain[vd, :])).astype(BF16)
        if own:
            for cut, out in zip(half_columns(r, width), (r.near, r.away)):
                out[...] = tn(r.gated[...], r.ow[:, cut])

    return c.run(name, body)


def feed(own, name, middle, top, shared, weights, after=()):
    inner_wt, linear_wt, down_w = weights
    features, width = inner_wt.shape
    blocks, rows = len(middle), shared.rows
    c = Call(blocks)
    c.scalars(info=shared.info)
    c.whole(gain=shared.second_gain, bias=shared.second_bias)
    c.pieces(m=middle)
    c.whole(iw=inner_wt, lw=linear_wt, dw=down_w)
    c.after(*after)
    c.temp(m_rows=((rows, width), F32))
    if own:
        c.whole(c=top)
        part = ((rows, width // 2), F32)
        c.result(two_near=part, two_away=part, ff_near=part, ff_away=part)
    else:
        c.pieces(c=top)
        c.temp(c_rows=((rows, width), F32))
    flat = ((rows, width), BF16)
    tall = ((features, rows), BF16)
    c.results(normed=flat, top=flat, hidden=tall, gi=tall, gl=tall)

    def body(r):
        place_pieces(r, r.m_rows, r.m, width)
        hat, unused = standard(r.m_rows[...], EPS, 1)
        r.normed[...] = (hat * r.gain[...] + r.bias[...]).astype(BF16)
        if own:
            r.top[...] = r.c[...]
        else:
            place_pieces(r, r.c_rows, r.c, width)
            r.top[...] = r.c_rows[...].astype(BF16)
        for at in range(0, features, VD):
            cut = pl.ds(at, VD)
            inner = nt(r.iw[cut, :], r.normed[...])
            linear = nt(r.lw[cut, :], r.normed[...])
            upstream = nt(r.dw[cut, :], r.top[...])
            cumulative = 0.5 * (1.0 + lax.erf(inner * 0.7071067811865476))
            gelu = inner * cumulative
            slope = cumulative + inner * jnp.exp(-0.5 * inner * inner) * 0.3989422804014327
            r.hidden[cut, :] = (gelu * linear).astype(BF16)
            r.gi[cut, :] = (upstream * linear * slope).astype(BF16)
            r.gl[cut, :] = (upstream * gelu).astype(BF16)
        if own:
            cuts = half_columns(r, width)
            for cut, out in zip(cuts, (r.two_near, r.two_away)):
                out[...] = tn(r.gi[...], r.iw[:, cut]) + tn(r.gl[...], r.lw[:, cut])
            for cut, out in zip(cuts, (r.ff_near, r.ff_away)):
                out[...] = tn(r.hidden[...], r.dw[:, cut])

    return c.run(name, body)


def add_sums(r, upstream, hat):
    @pl.when(pl.program_id(0) == 0)
    def _():
        r.gain_sum[...] = jnp.zeros(r.gain_sum.shape, F32)
        r.bias_sum[...] = jnp.zeros(r.bias_sum.shape, F32)

    r.gain_sum[...] += jnp.sum(upstream * hat, 0, keepdims=True)
    r.bias_sum[...] += jnp.sum(upstream, 0, keepdims=True)


def middle_back(middle, upstream, top, shared, after=()):
    rows, width = top.shape
    c = Call(4, rows)
    c.scalars(info=shared.info)
    c.whole(gain=shared.second_gain, top=top)
    c.pieces(m=middle, u=upstream)
    c.after(*after)
    flat = ((rows, width), F32)
    line = ((1, width), F32)
    part = ((rows // 4, width), F32)
    c.temp(m_rows=part, u_rows=part)
    c.result(grad=flat, half=((rows, width // 2), F32), gain_sum=line, bias_sum=line)
    c.result(quarter=((rows, width // 4), F32))

    def body(r):
        place_pieces(r, r.m_rows, r.m, width)
        place_pieces(r, r.u_rows, r.u, width)
        hat, inverse = standard(r.m_rows[...], EPS, 1)
        upstream = r.u_rows[...]
        add_sums(r, upstream, hat)
        r.grad[...] = r.top[...].astype(F32) + norm_back(
            upstream, hat, inverse, r.gain[...], 1
        )
        r.half[...] = r.grad[:, half_columns(r, width)[0]]
        n = width // 4
        at = (r.info[0] * 2 + r.info[1]) * n
        r.quarter[...] = r.grad[:, pl.ds(pl.multiple_of(at, n), n)]

    return c.run("middle_back", body)


def back(own, name, grad, state, document, shared, weights, heads, after=()):
    query_w, key_w, value_wt, gate_wt, out_w = weights
    width = query_w.shape[0]
    features = value_wt.shape[0]
    blocks, unused, rows = document.shape
    c = Call(blocks)
    c.scalars(info=shared.info, rates=shared.rates)
    c.whole(head_gain=shared.head_gain)
    c.cut(document=document)
    c.cut(q=state.q, k=state.k, v=state.v, s=state.s, g=state.g, hat=state.hat, inv=state.inv)
    c.whole(ow=out_w)
    c.after(*after)
    if own:
        c.whole(m=grad, qw=query_w, kw=key_w, vw=value_wt, gw=gate_wt)
        part = ((rows, width // 2), F32)
        c.result(near=part, away=part, head_sum=((features, 1), F32))
    else:
        c.pieces(m=grad)
        c.temp(m_rows=((rows, width), F32))
    wide = ((rows, heads * KD), BF16)
    tall = ((features, rows), BF16)
    c.results(gm=((rows, width), BF16), gq=wide, gk=wide, gv=tall, gg=tall)

    def body(r):
        if own:
            r.gm[...] = r.m[...].astype(BF16)
        else:
            place_pieces(r, r.m_rows, r.m, width)
            r.gm[...] = r.m_rows[...].astype(BF16)
        decay = decays(r, heads)
        for h in range(heads):
            kd = pl.ds(h * KD, KD)
            vd = pl.ds(h * VD, VD)
            grad_gated = nt(r.ow[vd, :], r.gm[...])
            gates = r.g[vd, :]
            head_hat = r.hat[vd, :]
            gain = r.head_gain[vd, :]
            sigma = jax.nn.sigmoid(gates)
            r.gg[vd, :] = (
                grad_gated * (head_hat * gain) * sigma * (1.0 + gates * (1.0 - sigma))
            ).astype(BF16)
            grad_normed = grad_gated * (gates * sigma)
            if own:
                r.head_sum[vd, :] = jnp.sum(grad_normed * head_hat, 1, keepdims=True)
            mixed = norm_back(grad_normed, head_hat, r.inv[h], gain, 0).astype(BF16)
            masked = (tn(mixed, r.v[vd, :]) * decay[h]).astype(BF16)
            r.gv[vd, :] = nn(mixed, r.s[h]).astype(BF16)
            r.gq[:, kd] = nn(masked, r.k[:, kd]).astype(BF16)
            r.gk[:, kd] = (tn(masked, r.q[:, kd]) * SCALE).astype(BF16)
        if own:
            for cut, out in zip(half_columns(r, width), (r.near, r.away)):
                out[...] = (
                    nt(r.gq[...], r.qw[cut, :])
                    + nt(r.gk[...], r.kw[cut, :])
                    + tn(r.gv[...], r.vw[:, cut])
                    + tn(r.gg[...], r.gw[:, cut])
                )

    return c.run(name, body)


def weigh(name, terms, which, after=()):
    arrays, specs, outs, out_specs = [], [], [], []
    ends = []
    for array in terms[0][0]:
        ends.append(array.shape[0] + (ends[-1] if ends else 0))

    def at(i, b):
        count = terms[0][0][i].shape[0]
        return jnp.clip(b - (ends[i] - count), 0, count - 1) if count > 1 else 0

    for lefts, rights, turned, size in terms:
        for i, left in enumerate(lefts):
            arrays.append(left)
            specs.append(
                pl.BlockSpec((None, left.shape[1], size), lambda b, w, i=i: (at(i, b), 0, w[0]))
            )
        for i, right in enumerate(rights):
            arrays.append(right)
            specs.append(
                pl.BlockSpec((None,) + right.shape[1:], lambda b, w, i=i: (at(i, b), 0, 0))
            )
        shape = (size, right.shape[2]) if turned else (right.shape[1], size)
        outs.append(jax.ShapeDtypeStruct(shape, F32))
        out_specs.append(pl.BlockSpec(shape, lambda b, w: (0, 0)))
    for array in after:
        arrays.append(array)
        specs.append(pl.BlockSpec(memory_space=pl.ANY))
    n = len(ends)

    def kernel(w, *refs):
        results = refs[len(arrays) :]
        b = pl.program_id(0)

        def pick(some):
            value = some[-1][...]
            for end, ref in zip(ends[-2::-1], some[-2::-1]):
                value = lax.select(b < end, ref[...], value)
            return value

        for i, result in enumerate(results):
            left = pick(refs[2 * n * i : 2 * n * i + n])
            right = pick(refs[2 * n * i + n : 2 * n * i + 2 * n])
            got = tn(left, right) if terms[i][2] else nn(right, left)
            result[...] = lax.select(b > 0, result[...], jnp.zeros_like(got)) + got

    return pl.pallas_call(
        kernel,
        grid_spec=pltpu.PrefetchScalarGridSpec(
            num_scalar_prefetch=1, grid=(ends[-1],), in_specs=specs, out_specs=out_specs
        ),
        out_shape=outs,
        cost_estimate=LIGHT,
        name=name,
    )(which, *arrays)


def joined(pieces, info, width, after=()):
    rows = pieces[0].shape[0]
    c = Call(4, rows)
    c.scalars(info=info)
    c.pieces(y=[[pieces]])
    c.after(*after)
    c.result(out=((rows, width), F32))
    return c.run("joined", lambda r: place_pieces(r, r.out, r.y, width)).out


def input_gradient(pieces, inputs, middle, info, gain, after=()):
    rows, width = inputs.shape
    c = Call(4, rows)
    c.scalars(info=info)
    c.whole(gain=gain, x=inputs, middle=middle)
    c.pieces(u=[[pieces]])
    c.after(*after)
    line = ((1, width), F32)
    c.result(out=((rows, width), F32), gain_sum=line, bias_sum=line)
    c.temp(u_rows=((rows // 4, width), F32))

    def body(r):
        place_pieces(r, r.u_rows, r.u, width)
        hat, inverse = standard(r.x[...].astype(F32), EPS, 1)
        upstream = r.u_rows[...]
        add_sums(r, upstream, hat)
        r.out[...] = r.middle[...] + norm_back(upstream, hat, inverse, r.gain[...], 1)

    return c.run("finish", body)


def make_body(dp, tp):
    hi_count = dp // BITS

    def permute(x, target):
        pairs = []
        for d in range(dp):
            for t in range(tp):
                to_d, to_t = target(d, t)
                pairs.append((d * tp + t, to_d * tp + to_t))
        return lax.ppermute(x, AXES, pairs)

    swap_core = lambda x: permute(x, lambda d, t: (d, t ^ 1))
    swap_row = lambda x: permute(x, lambda d, t: (d, t ^ 2))
    swap_dp = lambda x, bit: permute(x, lambda d, t: (d ^ bit, t))

    gate = lambda x, earlier: lax.optimization_barrier((x,) + tuple(earlier))[0] if earlier else x

    class Stages:
        def __init__(self):
            self.before, self.now, self.sends = [], [], 0
            self.spare, self.fresh = [], []

        def send(self, swap, x, free=False):
            got = swap(x if free else gate(x, self.before))
            self.now.append(got)
            self.sends += 1
            return got

        def ran(self, *arrays):
            self.now += arrays

        def later(self, x):
            slot = [x, None]
            self.fresh.append(slot)
            return slot

        def end(self, limit=5):
            while self.spare and self.sends < limit:
                slot = self.spare.pop(0)
                slot[1] = self.send(swap_core, slot[0])
            self.spare, self.fresh = self.spare + self.fresh, []
            self.before, self.now, self.sends = self.now, [], 0

    def body(
        inputs,
        document,
        query_weight,
        key_weight,
        value_weight,
        gate_weight,
        out_weight,
        inner_weight,
        linear_weight,
        down_weight,
        first_gain,
        first_bias,
        head_gain,
        second_gain,
        second_bias,
        cotangent,
    ):
        rows, width = inputs.shape
        share = width // dp
        heads = query_weight.shape[1] // KD
        d = lax.axis_index("dp")
        t = lax.axis_index("tensor")
        core = t % 2
        row = t // 2
        info = jnp.stack([core, row]).astype(jnp.int32)
        numbers = (t * heads + jnp.arange(heads)).astype(F32)
        shared = SimpleNamespace(
            info=info,
            rows=rows,
            rates=jnp.log1p(-jnp.exp2(-5.0 - numbers)),
            first_gain=first_gain[None],
            first_bias=first_bias[None],
            second_gain=second_gain[None],
            second_bias=second_bias[None],
            head_gain=head_gain[:, None],
        )
        attention = (query_weight, key_weight, value_weight.T, gate_weight.T, out_weight)
        hidden_layer = (inner_weight.T, linear_weight.T, down_weight)

        low = d % BITS

        def share_of(x, place):
            cuts = [
                lax.dynamic_slice_in_dim(x, (hi * BITS + place) * share, share, x.ndim - 1)
                for hi in range(hi_count)
            ]
            return jnp.concatenate(cuts, x.ndim - 1)

        def over_hi(x, axis):
            hi = d // BITS
            cut = lambda k: lax.dynamic_slice_in_dim(x, (hi ^ k) * share, share, axis)
            total = cut(0)
            for k in range(1, hi_count):
                total = total + swap_dp(cut(k), k * BITS)
            return total

        def product(name, terms, place, after=()):
            ready = []
            for lefts, rights, turned in terms:
                if hi_count > 1:
                    lefts = [share_of(left, place) for left in lefts]
                ready.append((lefts, rights, turned, hi_count * share))
            index = place if hi_count == 1 else place * 0
            return weigh(name, ready, index.reshape(1).astype(jnp.int32), after)

        def finished(mine, arrived, axis=1):
            total = gate(mine, at.before) + arrived
            return over_hi(total, axis) if hi_count > 1 else total

        def term(lefts, rights, turned=False):
            return (lefts, rights, turned)

        side = lambda x: swap_dp(x, SIDE)
        following = lambda x: swap_dp(x, NEXT)
        far = lambda x: swap_dp(x, FAR)
        stack = lambda *parts: jnp.concatenate(parts, 0)

        def half(array):
            return lax.dynamic_slice_in_dim(array, core * (width // 2), width // 2, 1).astype(F32)

        def quarter(halved):
            return lax.dynamic_slice_in_dim(halved, row * (width // 4), width // 4, 1)

        def pairs(*slots):
            return [[slot[0], slot[1]] for slot in slots]

        def quads(one, two):
            return [[one[0], two[0], one[1], two[1]]]

        own_doc = document[None, None]
        live = (document < DOCS_DEV)[:, None]
        top = jnp.where(live, cotangent, jnp.zeros((), BF16))
        top_quarter = quarter(half(top))
        input_half = half(inputs)
        k = rows // 4
        at = Stages()

        doc_side = at.send(side, document)
        doc_far = at.send(far, document)
        x_side = [at.later(at.send(side, input_half[: 2 * k]))]
        t_next = at.later(at.send(following, top_quarter))
        x_far = [None, at.later(at.send(far, input_half[2 * k : 3 * k]))]
        own = attend(True, "attend_own", inputs, own_doc, shared, attention, heads)
        at.ran(own.near)
        at.end(0)

        branch = own.near + at.send(swap_core, own.away)
        at.end(2)

        branch_row = at.send(swap_row, branch)
        doc_both = at.send(side, doc_far)
        x_side.append(at.later(at.send(side, input_half[2 * k :])))
        x_far[0] = at.later(at.send(far, input_half[: 2 * k]))
        at.end()
        middle = input_half + (branch + branch_row)

        middle_core = at.send(swap_core, middle)
        at.end(3)

        x_far.append(at.later(at.send(far, input_half[3 * k :])))
        x_both = [at.later(at.send(side, x_far[0][0]))]
        t_next_row = at.later(at.send(swap_row, t_next[0]))
        middle_own = [[[middle, middle_core]]]
        fed = feed(True, "feed_own", middle_own, top, shared, hidden_layer, at.before)
        at.ran(fed.two_near)
        at.end()

        two = fed.two_near + at.send(swap_core, fed.two_away)
        at.end(2)

        two_row = at.send(swap_row, two)
        m_next = at.later(at.send(following, quarter(middle)))
        m_far = at.later(at.send(far, quarter(middle)))
        x_both.append(at.later(at.send(side, stack(x_far[1][0], x_far[2][0]))))
        ff = fed.ff_near + at.send(swap_core, fed.ff_away)
        at.ran(ff)
        at.end()
        two = two + two_row

        two_core = at.send(swap_core, two)
        at.end(4)

        grad = middle_back(middle_own, [[[two, two_core]]], top, shared, at.before)
        at.ran(grad.grad)
        at.end(9)

        g_side = at.send(side, grad.half)
        g_far = at.send(far, grad.quarter)
        m_next_row = at.send(swap_row, m_next[0])
        m_far_row = at.send(swap_row, m_far[0])
        m_next_row, g_side, g_far, m_far_row = map(
            at.later, (m_next_row, g_side, g_far, m_far_row)
        )
        other_doc = jnp.stack([doc_side, doc_far, doc_both])[:, None]
        others = attend(
            False,
            "attend",
            [pairs(*x_side), pairs(*x_far), pairs(*x_both)],
            other_doc,
            shared,
            attention,
            heads,
            at.before,
        )
        at.ran(others.q)
        at.end()

        g_both = at.later(at.send(side, g_far[0]))
        g_far_row = at.later(at.send(swap_row, g_far[0]))
        m_both = at.later(at.send(following, m_far[0]))
        t_far = at.send(far, top_quarter[: 2 * k])
        backed = back(
            True, "back_own", grad.grad, own, own_doc, shared, attention, heads, at.before
        )
        at.ran(backed.near)
        at.end()

        g_both_row = at.send(swap_row, g_both[0])
        t_far = stack(t_far, at.send(far, top_quarter[2 * k :]))
        one = backed.near + at.send(swap_core, backed.away)
        first_fed = feed(
            False,
            "feed_next",
            [quads(m_next, m_next_row)],
            [quads(t_next, t_next_row)],
            shared,
            hidden_layer,
            at.before,
        )
        at.ran(first_fed.gi)
        at.end()
        t_far = at.later(t_far)

        g_both_row = [g_both_row, at.send(swap_core, g_both_row)]
        at.end(5)

        t_both = at.later(at.send(following, t_far[0]))
        m_both_row = at.later(at.send(swap_row, m_both[0]))
        t_far_row = at.later(at.send(swap_row, t_far[0]))
        other_backed = back(
            False,
            "back",
            [pairs(g_side), quads(g_far, g_far_row), quads(g_both, g_both_row)],
            others,
            other_doc,
            shared,
            attention,
            heads,
            at.before,
        )
        first_normed = [own.normed, others.normed]
        value_terms = [
            term([backed.gm, other_backed.gm], [own.gated, others.gated]),
            term(first_normed, [backed.gg, other_backed.gg]),
            term(first_normed, [backed.gv, other_backed.gv]),
        ]
        key_terms = [
            term(first_normed, [backed.gq, other_backed.gq], True),
            term(first_normed, [backed.gk, other_backed.gk], True),
        ]
        key_sent = product("key_partial", key_terms, low ^ NEXT, at.before)
        at.ran(other_backed.gq, key_sent[0])
        at.end()

        t_both_row = at.send(swap_row, t_both[0])
        key_came = [at.send(following, key_sent[0])]
        value_sent = product("value_partial", value_terms, low ^ NEXT, at.before)
        at.ran(value_sent[0], one)
        at.end(6)

        t_both_row = [t_both_row, at.send(swap_core, t_both_row)]
        at.end(4)

        value_came = [at.send(following, value_sent[0])]
        one_row = at.send(swap_row, one)
        other_fed = feed(
            False,
            "feed",
            [quads(m_far, m_far_row), quads(m_both, m_both_row)],
            [quads(t_far, t_far_row), quads(t_both, t_both_row)],
            shared,
            hidden_layer,
            at.before,
        )
        feds = [fed, first_fed, other_fed]
        second_normed = [f.normed for f in feds]
        mlp_terms = [
            term([f.top for f in feds], [f.hidden for f in feds]),
            term(second_normed, [f.gi for f in feds]),
            term(second_normed, [f.gl for f in feds]),
        ]
        mlp_sent = product("mlp_partial", mlp_terms, low ^ SIDE, at.before)
        at.ran(mlp_sent[0])
        at.end()
        one = one + one_row

        value_came.append(at.send(following, value_sent[1]))
        mlp_came = [at.send(side, mlp_sent[0])]
        one_core = at.send(swap_core, one)
        ff_row = at.send(swap_row, ff)
        value_mine = product("value_mine", value_terms, low, at.before)
        key_mine = product("key_mine", key_terms, low, at.before)
        mlp_mine = product("mlp_mine", mlp_terms, low, at.before)
        at.ran(value_mine[0], key_mine[0], mlp_mine[0])
        at.end()
        ff = middle + (ff + ff_row)

        value_came.append(at.send(following, value_sent[2]))
        mlp_came.append(at.send(side, mlp_sent[1]))
        ff_core = at.send(swap_core, ff)
        finish = input_gradient(
            [one, one_core],
            inputs,
            grad.grad,
            info,
            shared.first_gain,
            at.before,
        )
        sums = jnp.concatenate(
            [
                grad.gain_sum[0],
                grad.bias_sum[0],
                finish.gain_sum[0],
                finish.bias_sum[0],
                backed.head_sum[:, 0],
            ]
        )
        sums = sums + at.send(side, sums, free=True)
        at.ran(finish.out)
        at.end()

        mlp_came.append(at.send(side, mlp_sent[2]))
        key_came.append(at.send(following, key_sent[1]))
        outputs = joined([ff, ff_core], info, width, at.before)
        grad_down, grad_inner, grad_linear = map(finished, mlp_mine, mlp_came)
        grad_out, grad_gate, grad_value = map(finished, value_mine, value_came)
        grad_query, grad_key = [finished(a, b, 0) for a, b in zip(key_mine, key_came)]

        ready = (key_came[1], outputs, grad_down, grad_inner, grad_out, grad_gate, grad_value)
        sums_next, sums_far, sums_both = [
            swap_dp(gate(sums, ready), bit) for bit in (NEXT, FAR, NEXT | FAR)
        ]
        sums = (sums + sums_next) + (sums_far + sums_both)
        bit = BITS
        while bit < dp:
            sums = sums + swap_dp(sums, bit)
            bit *= 2
        vector = lambda i: sums[i * width : (i + 1) * width]
        return (
            outputs,
            finish.out,
            grad_query,
            grad_key,
            grad_value.T,
            grad_gate.T,
            grad_out,
            grad_inner.T,
            grad_linear.T,
            grad_down,
            vector(2),
            vector(3),
            sums[4 * width :],
            vector(0),
            vector(1),
        )

    return body


def solution(mesh):
    in_specs = (
        P("dp", None),
        P("dp"),
        P(None, "tensor"),
        P(None, "tensor"),
        P(None, "tensor"),
        P(None, "tensor"),
        P("tensor", None),
        P(None, "tensor"),
        P(None, "tensor"),
        P("tensor", None),
        P(),
        P(),
        P("tensor"),
        P(),
        P(),
        P("dp", None),
    )
    out_specs = (
        P("dp", None),
        P("dp", None),
        P("dp", "tensor"),
        P("dp", "tensor"),
        P("dp", "tensor"),
        P("dp", "tensor"),
        P("tensor", "dp"),
        P("dp", "tensor"),
        P("dp", "tensor"),
        P("tensor", "dp"),
        P(),
        P(),
        P("tensor"),
        P(),
        P(),
    )
    body = make_body(mesh.shape["dp"], mesh.shape["tensor"])
    return jax.shard_map(body, mesh=mesh, in_specs=in_specs, out_specs=out_specs, check_vma=False)
```

profile of v0, /device:TPU:0, one launch (start us, length us, event | category | flops | bytes accessed | tf_op | source)
XLA Modules:
  0.0 344.5 jit_solution(15643564802254624656)
XLA Ops:
  2.9 3.1 collective-permute-start.3
  14.1 12.6 %attend_own.1 = (f32[256,1024]{1,0:T(8,128)}, f32[256,1024]{1,0:T(8,128)}, bf16[1,256,2048]{2,1,0:T(8,128)(2,1)}, bf16[1,256,512]{2,1,0:T(8,128)(2,1)}, bf16[1,2...) custom-call(s32[2]{0:T(128)} %pad_add_fusion.1.refs_0_, ...), custom_call_target="tpu_custom_call" | custom-call | flops 1 | bytes 1 | tf_op jit(solution)/shard_map/attend_own/pallas_call | solution.py:130
  37.4 19.1 %collective-permute-done.7 = f32[256,1024]{1,0:T(8,128)S(1)} collective-permute-done((f32[256,1024]{1,0:T(8,128)S(1)}, f32[256,1024]{1,0:T(8,128)S(1)}, u32[]{:S(2)}, u32[]{:S(2)}) %collective-permute-start.7) | collective-permute-done | bytes 1048608 | tf_op jit(solution)/shard_map/ppermute | solution.py:530
  56.8 3.2 collective-permute-done.10.refs_17_
  60.5 3.2 collective-permute-done.13.refs_9_.refs_20_
  66.5 13.3 %feed_own.1 = (f32[256,1024]{1,0:T(8,128)}, f32[256,1024]{1,0:T(8,128)}, f32[256,1024]{1,0:T(8,128)}, f32[256,1024]{1,0:T(8,128)}, bf16[1,256,2048]{2,1,0:T(8,12...) custom-call(s32[2]{0:T(128)} %pad_add_fusion.1.refs_0_, ...), custom_call_target="tpu_custom_call" | custom-call | flops 1 | bytes 1 | tf_op jit(solution)/shard_map/feed_own/pallas_call | solution.py:130
  89.3 20.2 %collective-permute-done.22 = f32[256,1024]{1,0:T(8,128)S(1)} collective-permute-done((f32[256,1024]{1,0:T(8,128)S(1)}, f32[256,1024]{1,0:T(8,128)S(1)}, u32[]{:S(2)}, u32[]{:S(2)}) %collective-permute-start.22) | collective-permute-done | bytes 1048608 | tf_op jit(solution)/shard_map/ppermute | solution.py:530
  119.2 6.1 %middle_back.1 = (f32[256,2048]{1,0:T(8,128)}, f32[256,1024]{1,0:T(8,128)}, f32[1,2048]{1,0:T(1,128)}, f32[1,2048]{1,0:T(1,128)}, f32[256,512]{1,0:T(8,128)}) custom-call(s32[2]{0:T(128)} %pad_add_fusion.1.refs_0_, f32[1,2048]{1,0:T(1,128)} %bitcast.42, bf16[256,2048]{1,0:T(8,128)(2,1)} %copy-done.6, f32[256,1024]{1,0:T(8,128)} %copy-done, ...), custom_call_target="tpu_custom_call" | custom-call | flops 1 | bytes 1 | tf_op jit(solution)/shard_map/middle_back/pallas_call | solution.py:130
  131.1 21.5 %attend.1 = (bf16[3,256,2048]{2,1,0:T(8,128)(2,1)}, bf16[3,256,512]{2,1,0:T(8,128)(2,1)}, bf16[3,256,512]{2,1,0:T(8,128)(2,1)}, bf16[3,864,256]{2,1,0:T(8,128)(2...) custom-call(s32[2]{0:T(128)} %pad_add_fusion.1.refs_0_, ...), custom_call_target="tpu_custom_call" | custom-call | flops 1 | bytes 1 | tf_op jit(solution)/shard_map/attend/pallas_call | solution.py:130
  160.5 14.8 %back_own.1 = (f32[256,1024]{1,0:T(8,128)}, f32[256,1024]{1,0:T(8,128)}, f32[864,1]{1,0:T(8,128)}, bf16[1,256,2048]{2,1,0:T(8,128)(2,1)}, bf16[1,256,512]{2,1,0:...) custom-call(s32[2]{0:T(128)} %pad_add_fusion.1.refs_0_, ...), custom_call_target="tpu_custom_call" | custom-call | flops 1 | bytes 1 | tf_op jit(solution)/shard_map/back_own/pallas_call | solution.py:130
  177.9 10.4 %feed_next.1 = (bf16[1,256,2048]{2,1,0:T(8,128)(2,1)}, bf16[1,256,2048]{2,1,0:T(8,128)(2,1)}, bf16[1,864,256]{2,1,0:T(8,128)(2,1)}, bf16[1,864,256]{2,1,0:T(8,128)(2,1)}, bf16[1,864,256]{2,1,0:T(8,128)(2,1)}) custom-call(s32[2]{0:T(128)} %pad_add_fusion.1.refs_0_, f32[1,2048]{1,0:T(1,128)} %bitcast.43, f32[1,2048]{1,0:T(1,128)} %bitcast.46, ...), custom_call_target="tpu_custom_call" | custom-call | flops 1 | bytes 1 | tf_op jit(solution)/shard_map/feed_next/pallas_call | solution.py:130
  188.3 3.6 %collective-permute-done.42 = f32[128,512]{1,0:T(8,128)S(1)} collective-permute-done((f32[128,512]{1,0:T(8,128)}, f32[128,512]{1,0:T(8,128)S(1)}, u32[]{:S(2)}, u32[]{:S(2)}) %collective-permute-start.42) | collective-permute-done | bytes 262176 | tf_op jit(solution)/shard_map/ppermute | solution.py:530
  200.3 17.9 %back.1 = (bf16[3,256,2048]{2,1,0:T(8,128)(2,1)}, bf16[3,256,512]{2,1,0:T(8,128)(2,1)}, bf16[3,256,512]{2,1,0:T(8,128)(2,1)}, bf16[3,864,256]{2,1,0:T(8,128)(2,1)}, bf16[3,864,256]{2,1,0:T(8,128)(2,1)}) custom-call(s32[2]{0:T(128)} %pad_add_fusion.1.refs_0_, f32[2]{0:T(128)} %negate_log-plus-one_fusion.refs_1_, f32[864,1]{1,0:T(8,128)} %broadcast_in_dim.43.refs_4_.refs_2_, ...), custom_call_target="tpu_custom_call" | custom-call | flops 1 | bytes 1 | tf_op jit(solution)/shard_map/back/pallas_call | solution.py:130
  218.3 4.7 %key_partial.1 = (f32[256,512]{1,0:T(8,128)}, f32[256,512]{1,0:T(8,128)}) custom-call(s32[1]{0:T(128)} %bitcast.11.w, bf16[1,256,2048]{2,1,0:T(8,128)(2,1)} %get-tuple-element.234.refs_0_.refs_4_.refs_8_, bf16[3,256,2048]{2,1,0:T(8,128)(2,1)} %get-tuple-element.235.refs_1_.refs_5_.refs_9_, bf16[1,256,512]{2,1,0:T(8,128)(2,1)} %get-tuple-element.243.refs_2_, ...), custom_call_target="tpu_custom_call" | custom-call | flops 1 | bytes 1 | tf_op jit(solution)/shard_map/key_partial/pallas_call | solution.py:479
  228.4 6.5 %value_partial.1 = (f32[864,256]{1,0:T(8,128)}, f32[864,256]{1,0:T(8,128)}, f32[864,256]{1,0:T(8,128)}) custom-call(s32[1]{0:T(128)} %bitcast.11.w, bf16[1,256,2048]{2,1,0:T(8,128)(2,1)} %get-tuple-element.207.refs_0_, bf16[3,256,2048]{2,1,0:T(8,128)(2,1)} %get-tuple-element.231.refs_1_, bf16[1,864,256]{2,1,0:T(8,128)(2,1)} %get-tuple-element.232.refs_2_, ...), custom_call_target="tpu_custom_call" | custom-call | flops 1 | bytes 1 | tf_op jit(solution)/shard_map/value_partial/pallas_call | solution.py:479
  234.9 3.7 %collective-permute-done.55.refs_20_ = f32[256,512]{1,0:T(8,128)} collective-permute-done((f32[256,512]{1,0:T(8,128)}, f32[256,512]{1,0:T(8,128)}, u32[]{:S(2)}, u32[]{:S(2)}) %collective-permute-start.55) | collective-permute-done | bytes 524320 | tf_op jit(solution)/shard_map/ppermute | solution.py:530
  243.6 15.8 %feed.1 = (bf16[2,256,2048]{2,1,0:T(8,128)(2,1)}, bf16[2,256,2048]{2,1,0:T(8,128)(2,1)}, bf16[2,864,256]{2,1,0:T(8,128)(2,1)}, bf16[2,864,256]{2,1,0:T(8,128)(2,1)}, bf16[2,864,256]{2,1,0:T(8,128)(2,1)}) custom-call(s32[2]{0:T(128)} %pad_add_fusion.1.refs_0_, f32[1,2048]{1,0:T(1,128)} %bitcast.44, f32[1,2048]{1,0:T(1,128)} %bitcast.47, ...), custom_call_target="tpu_custom_call" | custom-call | flops 1 | bytes 1 | tf_op jit(solution)/shard_map/feed/pallas_call | solution.py:130
  259.4 7.0 %mlp_partial.1 = (f32[864,256]{1,0:T(8,128)}, f32[864,256]{1,0:T(8,128)}, f32[864,256]{1,0:T(8,128)}) custom-call(s32[1]{0:T(128)} %bitcast.15.w, bf16[1,256,2048]{2,1,0:T(8,128)(2,1)} %get-tuple-element.255.refs_0_, bf16[1,256,2048]{2,1,0:T(8,128)(2,1)} %get-tuple-element.256.refs_1_, bf16[2,256,2048]{2,1,0:T(8,128)(2,1)} %get-tuple-element.257.refs_2_, ...), custom_call_target="tpu_custom_call" | custom-call | flops 1 | bytes 1 | tf_op jit(solution)/shard_map/mlp_partial/pallas_call | solution.py:479
  272.5 7.1 %mlp_mine.1 = (f32[864,256]{1,0:T(8,128)}, f32[864,256]{1,0:T(8,128)}, f32[864,256]{1,0:T(8,128)}) custom-call(s32[1]{0:T(128)} %bitcast.16.w, bf16[1,256,2048]{2,1,0:T(8,128)(2,1)} %get-tuple-element.255.refs_0_, bf16[1,256,2048]{2,1,0:T(8,128)(2,1)} %get-tuple-element.256.refs_1_, bf16[2,256,2048]{2,1,0:T(8,128)(2,1)} %get-tuple-element.257.refs_2_, ...), custom_call_target="tpu_custom_call" | custom-call | flops 1 | bytes 1 | tf_op jit(solution)/shard_map/mlp_mine/pallas_call | solution.py:479
  279.6 6.5 %value_mine.1 = (f32[864,256]{1,0:T(8,128)}, f32[864,256]{1,0:T(8,128)}, f32[864,256]{1,0:T(8,128)}) custom-call(s32[1]{0:T(128)} %bitcast.16.w, bf16[1,256,2048]{2,1,0:T(8,128)(2,1)} %get-tuple-element.207.refs_0_, bf16[3,256,2048]{2,1,0:T(8,128)(2,1)} %get-tuple-element.231.refs_1_, bf16[1,864,256]{2,1,0:T(8,128)(2,1)} %get-tuple-element.232.refs_2_, ...), custom_call_target="tpu_custom_call" | custom-call | flops 1 | bytes 1 | tf_op jit(solution)/shard_map/value_mine/pallas_call | solution.py:479
  286.1 4.7 %key_mine.1 = (f32[256,512]{1,0:T(8,128)}, f32[256,512]{1,0:T(8,128)}) custom-call(s32[1]{0:T(128)} %bitcast.16.w, bf16[1,256,2048]{2,1,0:T(8,128)(2,1)} %get-tuple-element.234.refs_0_.refs_4_.refs_8_, bf16[3,256,2048]{2,1,0:T(8,128)(2,1)} %get-tuple-element.235.refs_1_.refs_5_.refs_9_, bf16[1,256,512]{2,1,0:T(8,128)(2,1)} %get-tuple-element.243.refs_2_, ...), custom_call_target="tpu_custom_call" | custom-call | flops 1 | bytes 1 | tf_op jit(solution)/shard_map/key_mine/pallas_call | solution.py:479
  298.0 5.4 %finish.1 = (f32[256,2048]{1,0:T(8,128)}, f32[1,2048]{1,0:T(1,128)}, f32[1,2048]{1,0:T(1,128)}) custom-call(s32[2]{0:T(128)} %pad_add_fusion.1.refs_0_, f32[1,2048]{1,0:T(1,128)} %bitcast.50, bf16[256,2048]{1,0:T(8,128)(2,1)} %refs_2_.1, f32[256,2048]{1,0:T(8,128)} %get-tuple-element.198.refs_10_.refs_17_.refs_3_, f32[256,1024]{1,0:T(8,128)} %add.104.refs_4_, ...), custom_call_target="tpu_custom_call" | custom-call | flops 1 | bytes 1 | tf_op jit(solution)/shard_map/finish/pallas_call | solution.py:130
  308.3 9.6 %collective-permute-done.70.refs_6_ = f32[9056]{0:T(1024)S(1)} collective-permute-done((f32[9056]{0:T(1024)}, f32[9056]{0:T(1024)S(1)}, u32[]{:S(2)}, u32[]{:S(2)}) %collective-permute-start.70) | collective-permute-done | bytes 36256 | tf_op jit(solution)/shard_map/ppermute | solution.py:530
  320.3 3.9 %joined.1 = f32[256,2048]{1,0:T(8,128)} custom-call(s32[2]{0:T(128)} %pad_add_fusion.1.refs_0_, f32[256,1024]{1,0:T(8,128)} %copy-done.20, f32[256,1024]{1,0:T(8,128)} %copy-done.17, f32[864,256]{1,0:T(8,128)} %copy-done.24, f32[864,256]{1,0:T(8,128)} %collective-permute-done.69.refs_4_, f32[256,1024]{1,0:T(8,128)} %copy-done.17, f32[9056]{0:T(1024)} %copy-done.60, ...), custom_call_target="tpu_custom_call" | custom-call | flops 1 | bytes 1 | tf_op jit(solution)/shard_map/joined/pallas_call | solution.py:130
  (320 shorter events, 118.5 us)
Async XLA Ops:
  2.9 23.9 %collective-permute-start.3 = (f32[256,512]{1,0:T(8,128)S(1)}, f32[256,512]{1,0:T(8,128)S(1)}, u32[]{:S(2)}, u32[]{:S(2)}) collective-permute-start(f32[256,512]{1,0:T(8,128)S(1)} %dynamic-slice_convert_fusion.1), channel_id=1, source_target_pairs={{0,8},{1,9},{2,10},{3,11},{4,12},{5,13},{6,14},{7,15},{8,0},{9,1},... | collective-permute-start | bytes 1572872 | tf_op jit(solution)/shard_map/ppermute | solution.py:530
  31.2 25.3 %collective-permute-start.7 = (f32[256,1024]{1,0:T(8,128)S(1)}, f32[256,1024]{1,0:T(8,128)S(1)}, u32[]{:S(2)}, u32[]{:S(2)}) collective-permute-start(f32[256,1024]{1,0:T(8,128)S(1)} %add.94), channel_id=1, source_target_pairs={{0,2},{1,3},{2,0},{3,1},{4,6},{5,7},{6,4},{7,5},{8,10},{9,11},{10,... | collective-permute-start | bytes 3145736 | tf_op jit(solution)/shard_map/ppermute | solution.py:530
  32.8 24.0 %collective-permute-start.9 = (f32[128,1024]{1,0:T(8,128)S(1)}, f32[128,1024]{1,0:T(8,128)S(1)}, u32[]{:S(2)}, u32[]{:S(2)}) collective-permute-start(f32[128,1024]{1,0:T(8,128)S(1)} %get-tuple-element.167), channel_id=1, source_target_pairs={{0,4},{1,5},{2,6},{3,7},{4,0},{5,1},{6,2},{7,3},{8,12},{9,13},{10,... | collective-permute-start | bytes 1572872 | tf_op jit(solution)/shard_map/ppermute | solution.py:530
  34.3 25.6 %collective-permute-start.10 = (f32[128,1024]{1,0:T(8,128)S(1)}, f32[128,1024]{1,0:T(8,128)}, u32[]{:S(2)}, u32[]{:S(2)}) collective-permute-start(f32[128,1024]{1,0:T(8,128)S(1)} %get-tuple-element.168), channel_id=1, source_target_pairs={{0,16},{1,17},{2,18},{3,19},{4,20},{5,21},{6,22},{7,23},{8,24},{9,... | collective-permute-start | bytes 1572872 | tf_op jit(solution)/shard_map/ppermute | solution.py:530
  84.2 25.3 %collective-permute-start.22 = (f32[256,1024]{1,0:T(8,128)S(1)}, f32[256,1024]{1,0:T(8,128)S(1)}, u32[]{:S(2)}, u32[]{:S(2)}) collective-permute-start(f32[256,1024]{1,0:T(8,128)S(1)} %add.99), channel_id=1, source_target_pairs={{0,2},{1,3},{2,0},{3,1},{4,6},{5,7},{6,4},{7,5},{8,10},{9,11},{10,... | collective-permute-start | bytes 3145736 | tf_op jit(solution)/shard_map/ppermute | solution.py:530
  85.6 24.1 %collective-permute-start.21 = (f32[256,1024]{1,0:T(8,128)S(1)}, f32[256,1024]{1,0:T(8,128)S(1)}, u32[]{:S(2)}, u32[]{:S(2)}) collective-permute-start(f32[256,1024]{1,0:T(8,128)S(1)} %copy-done.65), channel_id=1, source_target_pairs={{0,1},{1,0},{2,3},{3,2},{4,5},{5,4},{6,7},{7,6},{8,9},{9,8},{10,11... | collective-permute-start | bytes 3145736 | tf_op jit(solution)/shard_map/ppermute | solution.py:530
  85.8 26.6 %collective-permute-start.24 = (f32[256,512]{1,0:T(8,128)S(1)}, f32[256,512]{1,0:T(8,128)}, u32[]{:S(2)}, u32[]{:S(2)}) collective-permute-start(f32[256,512]{1,0:T(8,128)S(1)} %constant_dynamic-slice_fusion), channel_id=1, source_target_pairs={{0,16},{1,17},{2,18},{3,19},{4,20},{5,21},{6,22},{7,23},{8,24},{9,... | collective-permute-start | bytes 1572872 | tf_op jit(solution)/shard_map/ppermute | solution.py:530
  87.5 24.9 %collective-permute-start.23 = (f32[256,512]{1,0:T(8,128)S(1)}, f32[256,512]{1,0:T(8,128)S(1)}, u32[]{:S(2)}, u32[]{:S(2)}) collective-permute-start(f32[256,512]{1,0:T(8,128)S(1)} %constant_dynamic-slice_fusion), channel_id=1, source_target_pairs={{0,8},{1,9},{2,10},{3,11},{4,12},{5,13},{6,14},{7,15},{8,0},{9,1},... | collective-permute-start | bytes 1572872 | tf_op jit(solution)/shard_map/ppermute | solution.py:530
  87.8 24.6 %collective-permute-start.25 = (f32[128,1024]{1,0:T(8,128)S(1)}, f32[128,1024]{1,0:T(8,128)}, u32[]{:S(2)}, u32[]{:S(2)}) collective-permute-start(f32[128,1024]{1,0:T(8,128)S(1)} %pad_maximum_fusion), channel_id=1, source_target_pairs={{0,4},{1,5},{2,6},{3,7},{4,0},{5,1},{6,2},{7,3},{8,12},{9,13},{10,... | collective-permute-start | bytes 1572872 | tf_op jit(solution)/shard_map/ppermute | solution.py:530
  125.2 29.2 %collective-permute-start.32 = (f32[256,1024]{1,0:T(8,128)}, f32[256,1024]{1,0:T(8,128)S(1)}, u32[]{:S(2)}, u32[]{:S(2)}) collective-permute-start(f32[256,1024]{1,0:T(8,128)} %get-tuple-element.201), channel_id=1, source_target_pairs={{0,4},{1,5},{2,6},{3,7},{4,0},{5,1},{6,2},{7,3},{8,12},{9,13},{10,... | collective-permute-start | bytes 3145736 | tf_op jit(solution)/shard_map/ppermute | solution.py:530
  126.8 25.8 %collective-permute-start.34 = (f32[256,512]{1,0:T(8,128)}, f32[256,512]{1,0:T(8,128)S(1)}, u32[]{:S(2)}, u32[]{:S(2)}) collective-permute-start(f32[256,512]{1,0:T(8,128)} %copy-done.55), channel_id=1, source_target_pairs={{0,2},{1,3},{2,0},{3,1},{4,6},{5,7},{6,4},{7,5},{8,10},{9,11},{10,... | collective-permute-start | bytes 1572872 | tf_op jit(solution)/shard_map/ppermute | solution.py:530
  127.3 25.3 %collective-permute-start.35 = (f32[256,512]{1,0:T(8,128)}, f32[256,512]{1,0:T(8,128)S(1)}, u32[]{:S(2)}, u32[]{:S(2)}) collective-permute-start(f32[256,512]{1,0:T(8,128)} %collective-permute-done.24.refs_3_), channel_id=1, source_target_pairs={{0,2},{1,3},{2,0},{3,1},{4,6},{5,7},{6,4},{7,5},{8,10},{9,11},{10,... | collective-permute-start | bytes 1572872 | tf_op jit(solution)/shard_map/ppermute | solution.py:530
  128.8 25.6 %collective-permute-start.33 = (f32[256,512]{1,0:T(8,128)}, f32[256,512]{1,0:T(8,128)}, u32[]{:S(2)}, u32[]{:S(2)}) collective-permute-start(f32[256,512]{1,0:T(8,128)} %get-tuple-element.203), channel_id=1, source_target_pairs={{0,16},{1,17},{2,18},{3,19},{4,20},{5,21},{6,22},{7,23},{8,24},{9,... | collective-permute-start | bytes 1572872 | tf_op jit(solution)/shard_map/ppermute | solution.py:530
  198.1 24.9 %collective-permute-start.54 = (f32[256,512]{1,0:T(8,128)}, f32[256,512]{1,0:T(8,128)S(1)}, u32[]{:S(2)}, u32[]{:S(2)}) collective-permute-start(f32[256,512]{1,0:T(8,128)} %constant_dynamic-update-slice_fusion.refs_15_), channel_id=1, source_target_pairs={{0,1},{1,0},{2,3},{3,2},{4,5},{5,4},{6,7},{7,6},{8,9},{9,8},{10,11... | collective-permute-start | bytes 1572872 | tf_op jit(solution)/shard_map/ppermute | solution.py:530
  198.3 24.8 %collective-permute-start.53 = (f32[256,512]{1,0:T(8,128)}, f32[256,512]{1,0:T(8,128)}, u32[]{:S(2)}, u32[]{:S(2)}) collective-permute-start(f32[256,512]{1,0:T(8,128)} %constant_dynamic-update-slice_fusion.refs_15_), channel_id=1, source_target_pairs={{0,2},{1,3},{2,0},{3,1},{4,6},{5,7},{6,4},{7,5},{8,10},{9,11},{10,... | collective-permute-start | bytes 1572872 | tf_op jit(solution)/shard_map/ppermute | solution.py:530
  199.8 23.2 %collective-permute-start.51 = (f32[256,512]{1,0:T(8,128)}, f32[256,512]{1,0:T(8,128)}, u32[]{:S(2)}, u32[]{:S(2)}) collective-permute-start(f32[256,512]{1,0:T(8,128)} %constant_dynamic-update-slice_fusion.refs_15_), channel_id=1, source_target_pairs={{0,8},{1,9},{2,10},{3,11},{4,12},{5,13},{6,14},{7,15},{8,0},{9,1},... | collective-permute-start | bytes 1572872 | tf_op jit(solution)/shard_map/ppermute | solution.py:530
  199.8 24.2 %collective-permute-start.52 = (f32[256,512]{1,0:T(8,128)}, f32[256,512]{1,0:T(8,128)}, u32[]{:S(2)}, u32[]{:S(2)}) collective-permute-start(f32[256,512]{1,0:T(8,128)} %copy-done.29), channel_id=1, source_target_pairs={{0,2},{1,3},{2,0},{3,1},{4,6},{5,7},{6,4},{7,5},{8,10},{9,11},{10,... | collective-permute-start | bytes 1572872 | tf_op jit(solution)/shard_map/ppermute | solution.py:530
  242.0 25.4 %collective-permute-start.62 = (f32[256,1024]{1,0:T(8,128)}, f32[256,1024]{1,0:T(8,128)S(1)}, u32[]{:S(2)}, u32[]{:S(2)}) collective-permute-start(f32[256,1024]{1,0:T(8,128)} %add.101), channel_id=1, source_target_pairs={{0,2},{1,3},{2,0},{3,1},{4,6},{5,7},{6,4},{7,5},{8,10},{9,11},{10,... | collective-permute-start | bytes 3145736 | tf_op jit(solution)/shard_map/ppermute | solution.py:530
  242.5 23.9 %collective-permute-start.61 = (f32[864,256]{1,0:T(8,128)}, f32[864,256]{1,0:T(8,128)S(1)}, u32[]{:S(2)}, u32[]{:S(2)}) collective-permute-start(f32[864,256]{1,0:T(8,128)} %get-tuple-element.253), channel_id=1, source_target_pairs={{0,8},{1,9},{2,10},{3,11},{4,12},{5,13},{6,14},{7,15},{8,0},{9,1},... | collective-permute-start | bytes 2654216 | tf_op jit(solution)/shard_map/ppermute | solution.py:530
  267.4 24.7 %collective-permute-start.63 = (f32[256,1024]{1,0:T(8,128)}, f32[256,1024]{1,0:T(8,128)}, u32[]{:S(2)}, u32[]{:S(2)}) collective-permute-start(f32[256,1024]{1,0:T(8,128)} %add.97), channel_id=1, source_target_pairs={{0,2},{1,3},{2,0},{3,1},{4,6},{5,7},{6,4},{7,5},{8,10},{9,11},{10,... | collective-permute-start | bytes 3145736 | tf_op jit(solution)/shard_map/ppermute | solution.py:530
  270.4 23.5 %collective-permute-start.66 = (f32[256,1024]{1,0:T(8,128)}, f32[256,1024]{1,0:T(8,128)}, u32[]{:S(2)}, u32[]{:S(2)}) collective-permute-start(f32[256,1024]{1,0:T(8,128)} %add.104.refs_4_), channel_id=1, source_target_pairs={{0,1},{1,0},{2,3},{3,2},{4,5},{5,4},{6,7},{7,6},{8,9},{9,8},{10,11... | collective-permute-start | bytes 3145736 | tf_op jit(solution)/shard_map/ppermute | solution.py:530
  270.4 23.5 %collective-permute-start.64 = (f32[864,256]{1,0:T(8,128)S(1)}, f32[864,256]{1,0:T(8,128)}, u32[]{:S(2)}, u32[]{:S(2)}) collective-permute-start(f32[864,256]{1,0:T(8,128)S(1)} %copy-done.66), channel_id=1, source_target_pairs={{0,8},{1,9},{2,10},{3,11},{4,12},{5,13},{6,14},{7,15},{8,0},{9,1},... | collective-permute-start | bytes 2654216 | tf_op jit(solution)/shard_map/ppermute | solution.py:530
  293.9 24.0 %collective-permute-start.67 = (f32[256,1024]{1,0:T(8,128)S(1)}, f32[256,1024]{1,0:T(8,128)S(1)}, u32[]{:S(2)}, u32[]{:S(2)}) collective-permute-start(f32[256,1024]{1,0:T(8,128)S(1)} %add_add_fusion.refs_1_), channel_id=1, source_target_pairs={{0,1},{1,0},{2,3},{3,2},{4,5},{5,4},{6,7},{7,6},{8,9},{9,8},{10,11... | collective-permute-start | bytes 3145736 | tf_op jit(solution)/shard_map/ppermute | solution.py:530
  294.0 23.9 %collective-permute-start.68 = (f32[864,256]{1,0:T(8,128)}, f32[864,256]{1,0:T(8,128)S(1)}, u32[]{:S(2)}, u32[]{:S(2)}) collective-permute-start(f32[864,256]{1,0:T(8,128)} %get-tuple-element.280), channel_id=1, source_target_pairs={{0,8},{1,9},{2,10},{3,11},{4,12},{5,13},{6,14},{7,15},{8,0},{9,1},... | collective-permute-start | bytes 2654216 | tf_op jit(solution)/shard_map/ppermute | solution.py:530
  (119 other events, 1086.6 us)
where the time goes:
time: 351 us; the launch traced here: 344 us
  Pallas kernels  158 us (45%)
  waiting for transfers between devices  81.8 us (23%)
  starting transfers between devices  57.6 us (16%)
  other arithmetic  29.1 us (8%)
  local copies, waits for them, and re-layouts  15.7 us (4%)
    pallas_call x10, Pallas kernels, run(): pl.pallas_call(kernel, grid=(self.blocks,), in_specs=self.specs, out_spec...  122 us
    ppermute x76, waiting for transfers between devices, permute(): return lax.ppermute(x, AXES, pairs)  81.8 us
    ppermute x76, starting transfers between devices, permute(): return lax.ppermute(x, AXES, pairs)  57.6 us
    pallas_call x6, Pallas kernels, weigh(): pl.pallas_call(kernel, grid_spec=pltpu.PrefetchScalarGridSpec(num_scalar_...  36.5 us
    add x7, other arithmetic, finished(): total = gate(mine, at.before) + arrived  11.7 us
    unnamed x139, local copies, waits for them, and re-layouts  8.01 us
  transfers between devices with their start and end apart: 76, of which 21 were waited for; matrix products, arithmetic and copies ran while one was open for 11% of the time, Pallas kernels for 46%

commit v1 on v0

--- a/solution.py
+++ b/solution.py
@@ -197,14 +197,14 @@
     return jnp.broadcast_to(across, (rows, rows)).T
 
 
-def decays(r, heads):
+def decays(r):
     down = downwards(r)
     rows = down.shape[0]
     n = lax.broadcasted_iota(jnp.int32, (rows, rows), 0)
     m = lax.broadcasted_iota(jnp.int32, (rows, rows), 1)
     allowed = (n >= m) & (down == r.document[...].astype(F32))
     spread = jnp.where(allowed, (n - m).astype(F32), 0.0)
-    return [jnp.where(allowed, jnp.exp(spread * r.rates[h]), 0.0) for h in range(heads)]
+    return lambda h: jnp.where(allowed, jnp.exp(spread * r.rates[h]), 0.0)
 
 
 def half_columns(r, width):
@@ -258,11 +258,11 @@
         r.k[...] = (nn(normed, r.kw[...]) * SCALE).astype(BF16)
         r.v[...] = nt(r.vw[...], normed).astype(BF16)
         r.g[...] = nt(r.gw[...], normed)
-        decay = decays(r, heads)
+        decay = decays(r)
         for h in range(heads):
             kd = pl.ds(h * KD, KD)
             vd = pl.ds(h * VD, VD)
-            score = (nt(r.q[:, kd], r.k[:, kd]) * decay[h]).astype(BF16)
+            score = (nt(r.q[:, kd], r.k[:, kd]) * decay(h)).astype(BF16)
             r.s[h] = score
             head_hat, head_inv = standard(nt(r.v[vd, :], score), HEAD_EPS, 0)
             r.hat[vd, :] = head_hat
@@ -308,8 +308,7 @@
         else:
             place_pieces(r, r.c_rows, r.c, width)
             r.top[...] = r.c_rows[...].astype(BF16)
-        for at in range(0, features, VD):
-            cut = pl.ds(at, VD)
+        def units(cut):
             inner = nt(r.iw[cut, :], r.normed[...])
             linear = nt(r.lw[cut, :], r.normed[...])
             upstream = nt(r.dw[cut, :], r.top[...])
@@ -319,6 +318,8 @@
             r.hidden[cut, :] = (gelu * linear).astype(BF16)
             r.gi[cut, :] = (upstream * linear * slope).astype(BF16)
             r.gl[cut, :] = (upstream * gelu).astype(BF16)
+
+        by_rows(features, VD, units)
         if own:
             cuts = half_columns(r, width)
             for cut, out in zip(cuts, (r.two_near, r.two_away)):
@@ -399,10 +400,11 @@
         else:
             place_pieces(r, r.m_rows, r.m, width)
             r.gm[...] = r.m_rows[...].astype(BF16)
-        decay = decays(r, heads)
-        for h in range(heads):
-            kd = pl.ds(h * KD, KD)
-            vd = pl.ds(h * VD, VD)
+        decay = decays(r)
+        @pl.loop(0, heads)
+        def _(h):
+            kd = pl.ds(pl.multiple_of(h * KD, KD), KD)
+            vd = pl.ds(pl.multiple_of(h * VD, VD), VD)
             grad_gated = nt(r.ow[vd, :], r.gm[...])
             gates = r.g[vd, :]
             head_hat = r.hat[vd, :]
@@ -415,7 +417,7 @@
             if own:
                 r.head_sum[vd, :] = jnp.sum(grad_normed * head_hat, 1, keepdims=True)
             mixed = norm_back(grad_normed, head_hat, r.inv[h], gain, 0).astype(BF16)
-            masked = (tn(mixed, r.v[vd, :]) * decay[h]).astype(BF16)
+            masked = (tn(mixed, r.v[vd, :]) * decay(h)).astype(BF16)
             r.gv[vd, :] = nn(mixed, r.s[h]).astype(BF16)
             r.gq[:, kd] = nn(masked, r.k[:, kd]).astype(BF16)
             r.gk[:, kd] = (tn(masked, r.q[:, kd]) * SCALE).astype(BF16)

time: 351 us -> 352 us (level)
  transfers between devices with their start and end apart: 76 -> 76, of which waited for: 21 -> 19; matrix products, arithmetic and copies ran while one was open for 11% -> 11% of each run, Pallas kernels for 46% -> 46%
where the time goes in v1:
time: 352 us; the launch traced here: 346 us
  Pallas kernels  160 us (45%)
  waiting for transfers between devices  80.3 us (23%)
  starting transfers between devices  58.6 us (17%)
  other arithmetic  29.2 us (8%)
  local copies, waits for them, and re-layouts  15.7 us (4%)
    pallas_call x10, Pallas kernels, run(): pl.pallas_call(kernel, grid=(self.blocks,), in_specs=self.specs, out_spec...  124 us
    ppermute x76, waiting for transfers between devices, permute(): return lax.ppermute(x, AXES, pairs)  80.3 us
    ppermute x76, starting transfers between devices, permute(): return lax.ppermute(x, AXES, pairs)  58.6 us
    pallas_call x6, Pallas kernels, weigh(): pl.pallas_call(kernel, grid_spec=pltpu.PrefetchScalarGridSpec(num_scalar_...  36.5 us
    add x7, other arithmetic, finished(): total = gate(mine, at.before) + arrived  11.7 us
    unnamed x139, local copies, waits for them, and re-layouts  8.01 us
  transfers between devices with their start and end apart: 76, of which 19 were waited for; matrix products, arithmetic and copies ran while one was open for 11% of the time, Pallas kernels for 46%

profile of v1, /device:TPU:0, one launch (start us, length us, event | category | flops | bytes accessed | tf_op | source)
XLA Modules:
  0.0 346.1 jit_solution(2170889261899731215)
XLA Ops:
  2.9 3.1 collective-permute-start.3
  14.1 12.6 %attend_own.1 = (f32[256,1024]{1,0:T(8,128)}, f32[256,1024]{1,0:T(8,128)}, bf16[1,256,2048]{2,1,0:T(8,128)(2,1)}, bf16[1,256,512]{2,1,0:T(8,128)(2,1)}, bf16[1,2...) custom-call(s32[2]{0:T(128)} %pad_add_fusion.1.refs_0_, ...), custom_call_target="tpu_custom_call" | custom-call | flops 1 | bytes 1 | tf_op jit(solution)/shard_map/attend_own/pallas_call | solution.py:130
  37.4 19.1 %collective-permute-done.7 = f32[256,1024]{1,0:T(8,128)S(1)} collective-permute-done((f32[256,1024]{1,0:T(8,128)S(1)}, f32[256,1024]{1,0:T(8,128)S(1)}, u32[]{:S(2)}, u32[]{:S(2)}) %collective-permute-start.7) | collective-permute-done | bytes 1048608 | tf_op jit(solution)/shard_map/ppermute | solution.py:532
  56.8 3.2 collective-permute-done.10.refs_17_
  60.5 3.2 collective-permute-done.13.refs_9_.refs_20_
  66.5 13.9 %feed_own.1 = (f32[256,1024]{1,0:T(8,128)}, f32[256,1024]{1,0:T(8,128)}, f32[256,1024]{1,0:T(8,128)}, f32[256,1024]{1,0:T(8,128)}, bf16[1,256,2048]{2,1,0:T(8,12...) custom-call(s32[2]{0:T(128)} %pad_add_fusion.1.refs_0_, ...), custom_call_target="tpu_custom_call" | custom-call | flops 1 | bytes 1 | tf_op jit(solution)/shard_map/feed_own/pallas_call | solution.py:130
  89.9 20.2 %collective-permute-done.22 = f32[256,1024]{1,0:T(8,128)S(1)} collective-permute-done((f32[256,1024]{1,0:T(8,128)S(1)}, f32[256,1024]{1,0:T(8,128)S(1)}, u32[]{:S(2)}, u32[]{:S(2)}) %collective-permute-start.22) | collective-permute-done | bytes 1048608 | tf_op jit(solution)/shard_map/ppermute | solution.py:532
  119.2 6.1 %middle_back.1 = (f32[256,2048]{1,0:T(8,128)}, f32[256,1024]{1,0:T(8,128)}, f32[1,2048]{1,0:T(1,128)}, f32[1,2048]{1,0:T(1,128)}, f32[256,512]{1,0:T(8,128)}) custom-call(s32[2]{0:T(128)} %pad_add_fusion.1.refs_0_, f32[1,2048]{1,0:T(1,128)} %bitcast.42, bf16[256,2048]{1,0:T(8,128)(2,1)} %copy-done.6, f32[256,1024]{1,0:T(8,128)} %copy-done, ...), custom_call_target="tpu_custom_call" | custom-call | flops 1 | bytes 1 | tf_op jit(solution)/shard_map/middle_back/pallas_call | solution.py:130
  131.7 21.3 %attend.1 = (bf16[3,256,2048]{2,1,0:T(8,128)(2,1)}, bf16[3,256,512]{2,1,0:T(8,128)(2,1)}, bf16[3,256,512]{2,1,0:T(8,128)(2,1)}, bf16[3,864,256]{2,1,0:T(8,128)(2...) custom-call(s32[2]{0:T(128)} %pad_add_fusion.1.refs_0_, ...), custom_call_target="tpu_custom_call" | custom-call | flops 1 | bytes 1 | tf_op jit(solution)/shard_map/attend/pallas_call | solution.py:130
  160.6 15.1 %back_own.1 = (f32[256,1024]{1,0:T(8,128)}, f32[256,1024]{1,0:T(8,128)}, f32[864,1]{1,0:T(8,128)}, bf16[1,256,2048]{2,1,0:T(8,128)(2,1)}, bf16[1,256,512]{2,1,0:...) custom-call(s32[2]{0:T(128)} %pad_add_fusion.1.refs_0_, ...), custom_call_target="tpu_custom_call" | custom-call | flops 1 | bytes 1 | tf_op jit(solution)/shard_map/back_own/pallas_call | solution.py:130
  177.9 10.7 %feed_next.1 = (bf16[1,256,2048]{2,1,0:T(8,128)(2,1)}, bf16[1,256,2048]{2,1,0:T(8,128)(2,1)}, bf16[1,864,256]{2,1,0:T(8,128)(2,1)}, bf16[1,864,256]{2,1,0:T(8,128)(2,1)}, bf16[1,864,256]{2,1,0:T(8,128)(2,1)}) custom-call(s32[2]{0:T(128)} %pad_add_fusion.1.refs_0_, f32[1,2048]{1,0:T(1,128)} %bitcast.43, f32[1,2048]{1,0:T(1,128)} %bitcast.46, ...), custom_call_target="tpu_custom_call" | custom-call | flops 1 | bytes 1 | tf_op jit(solution)/shard_map/feed_next/pallas_call | solution.py:130
  188.5 4.0 %collective-permute-done.42 = f32[128,512]{1,0:T(8,128)S(1)} collective-permute-done((f32[128,512]{1,0:T(8,128)}, f32[128,512]{1,0:T(8,128)S(1)}, u32[]{:S(2)}, u32[]{:S(2)}) %collective-permute-start.42) | collective-permute-done | bytes 262176 | tf_op jit(solution)/shard_map/ppermute | solution.py:532
  201.0 17.5 %back.1 = (bf16[3,256,2048]{2,1,0:T(8,128)(2,1)}, bf16[3,256,512]{2,1,0:T(8,128)(2,1)}, bf16[3,256,512]{2,1,0:T(8,128)(2,1)}, bf16[3,864,256]{2,1,0:T(8,128)(2,1)}, bf16[3,864,256]{2,1,0:T(8,128)(2,1)}) custom-call(s32[2]{0:T(128)} %pad_add_fusion.1.refs_0_, f32[2]{0:T(128)} %negate_log-plus-one_fusion.refs_1_, f32[864,1]{1,0:T(8,128)} %broadcast_in_dim.43.refs_4_.refs_2_, ...), custom_call_target="tpu_custom_call" | custom-call | flops 1 | bytes 1 | tf_op jit(solution)/shard_map/back/pallas_call | solution.py:130
  218.5 4.7 %key_partial.1 = (f32[256,512]{1,0:T(8,128)}, f32[256,512]{1,0:T(8,128)}) custom-call(s32[1]{0:T(128)} %bitcast.11.w, bf16[1,256,2048]{2,1,0:T(8,128)(2,1)} %get-tuple-element.234.refs_0_.refs_4_.refs_8_, bf16[3,256,2048]{2,1,0:T(8,128)(2,1)} %get-tuple-element.235.refs_1_.refs_5_.refs_9_, bf16[1,256,512]{2,1,0:T(8,128)(2,1)} %get-tuple-element.243.refs_2_, ...), custom_call_target="tpu_custom_call" | custom-call | flops 1 | bytes 1 | tf_op jit(solution)/shard_map/key_partial/pallas_call | solution.py:481
  227.9 6.5 %value_partial.1 = (f32[864,256]{1,0:T(8,128)}, f32[864,256]{1,0:T(8,128)}, f32[864,256]{1,0:T(8,128)}) custom-call(s32[1]{0:T(128)} %bitcast.11.w, bf16[1,256,2048]{2,1,0:T(8,128)(2,1)} %get-tuple-element.207.refs_0_, bf16[3,256,2048]{2,1,0:T(8,128)(2,1)} %get-tuple-element.231.refs_1_, bf16[1,864,256]{2,1,0:T(8,128)(2,1)} %get-tuple-element.232.refs_2_, ...), custom_call_target="tpu_custom_call" | custom-call | flops 1 | bytes 1 | tf_op jit(solution)/shard_map/value_partial/pallas_call | solution.py:481
  234.4 4.9 %collective-permute-done.55.refs_20_ = f32[256,512]{1,0:T(8,128)} collective-permute-done((f32[256,512]{1,0:T(8,128)}, f32[256,512]{1,0:T(8,128)}, u32[]{:S(2)}, u32[]{:S(2)}) %collective-permute-start.55) | collective-permute-done | bytes 524320 | tf_op jit(solution)/shard_map/ppermute | solution.py:532
  243.8 17.2 %feed.1 = (bf16[2,256,2048]{2,1,0:T(8,128)(2,1)}, bf16[2,256,2048]{2,1,0:T(8,128)(2,1)}, bf16[2,864,256]{2,1,0:T(8,128)(2,1)}, bf16[2,864,256]{2,1,0:T(8,128)(2,1)}, bf16[2,864,256]{2,1,0:T(8,128)(2,1)}) custom-call(s32[2]{0:T(128)} %pad_add_fusion.1.refs_0_, f32[1,2048]{1,0:T(1,128)} %bitcast.44, f32[1,2048]{1,0:T(1,128)} %bitcast.47, ...), custom_call_target="tpu_custom_call" | custom-call | flops 1 | bytes 1 | tf_op jit(solution)/shard_map/feed/pallas_call | solution.py:130
  261.0 7.0 %mlp_partial.1 = (f32[864,256]{1,0:T(8,128)}, f32[864,256]{1,0:T(8,128)}, f32[864,256]{1,0:T(8,128)}) custom-call(s32[1]{0:T(128)} %bitcast.15.w, bf16[1,256,2048]{2,1,0:T(8,128)(2,1)} %get-tuple-element.255.refs_0_, bf16[1,256,2048]{2,1,0:T(8,128)(2,1)} %get-tuple-element.256.refs_1_, bf16[2,256,2048]{2,1,0:T(8,128)(2,1)} %get-tuple-element.257.refs_2_, ...), custom_call_target="tpu_custom_call" | custom-call | flops 1 | bytes 1 | tf_op jit(solution)/shard_map/mlp_partial/pallas_call | solution.py:481
  274.1 7.1 %mlp_mine.1 = (f32[864,256]{1,0:T(8,128)}, f32[864,256]{1,0:T(8,128)}, f32[864,256]{1,0:T(8,128)}) custom-call(s32[1]{0:T(128)} %bitcast.16.w, bf16[1,256,2048]{2,1,0:T(8,128)(2,1)} %get-tuple-element.255.refs_0_, bf16[1,256,2048]{2,1,0:T(8,128)(2,1)} %get-tuple-element.256.refs_1_, bf16[2,256,2048]{2,1,0:T(8,128)(2,1)} %get-tuple-element.257.refs_2_, ...), custom_call_target="tpu_custom_call" | custom-call | flops 1 | bytes 1 | tf_op jit(solution)/shard_map/mlp_mine/pallas_call | solution.py:481
  281.2 6.5 %value_mine.1 = (f32[864,256]{1,0:T(8,128)}, f32[864,256]{1,0:T(8,128)}, f32[864,256]{1,0:T(8,128)}) custom-call(s32[1]{0:T(128)} %bitcast.16.w, bf16[1,256,2048]{2,1,0:T(8,128)(2,1)} %get-tuple-element.207.refs_0_, bf16[3,256,2048]{2,1,0:T(8,128)(2,1)} %get-tuple-element.231.refs_1_, bf16[1,864,256]{2,1,0:T(8,128)(2,1)} %get-tuple-element.232.refs_2_, ...), custom_call_target="tpu_custom_call" | custom-call | flops 1 | bytes 1 | tf_op jit(solution)/shard_map/value_mine/pallas_call | solution.py:481
  287.7 4.7 %key_mine.1 = (f32[256,512]{1,0:T(8,128)}, f32[256,512]{1,0:T(8,128)}) custom-call(s32[1]{0:T(128)} %bitcast.16.w, bf16[1,256,2048]{2,1,0:T(8,128)(2,1)} %get-tuple-element.234.refs_0_.refs_4_.refs_8_, bf16[3,256,2048]{2,1,0:T(8,128)(2,1)} %get-tuple-element.235.refs_1_.refs_5_.refs_9_, bf16[1,256,512]{2,1,0:T(8,128)(2,1)} %get-tuple-element.243.refs_2_, ...), custom_call_target="tpu_custom_call" | custom-call | flops 1 | bytes 1 | tf_op jit(solution)/shard_map/key_mine/pallas_call | solution.py:481
  300.3 5.4 %finish.1 = (f32[256,2048]{1,0:T(8,128)}, f32[1,2048]{1,0:T(1,128)}, f32[1,2048]{1,0:T(1,128)}) custom-call(s32[2]{0:T(128)} %pad_add_fusion.1.refs_0_, f32[1,2048]{1,0:T(1,128)} %bitcast.50, bf16[256,2048]{1,0:T(8,128)(2,1)} %refs_2_.1, f32[256,2048]{1,0:T(8,128)} %get-tuple-element.198.refs_10_.refs_17_.refs_3_, f32[256,1024]{1,0:T(8,128)} %add.104.refs_4_, ...), custom_call_target="tpu_custom_call" | custom-call | flops 1 | bytes 1 | tf_op jit(solution)/shard_map/finish/pallas_call | solution.py:130
  309.5 9.6 %collective-permute-done.70.refs_6_ = f32[9056]{0:T(1024)S(1)} collective-permute-done((f32[9056]{0:T(1024)}, f32[9056]{0:T(1024)S(1)}, u32[]{:S(2)}, u32[]{:S(2)}) %collective-permute-start.70) | collective-permute-done | bytes 36256 | tf_op jit(solution)/shard_map/ppermute | solution.py:532
  322.2 3.9 %joined.1 = f32[256,2048]{1,0:T(8,128)} custom-call(s32[2]{0:T(128)} %pad_add_fusion.1.refs_0_, f32[256,1024]{1,0:T(8,128)} %copy-done.20, f32[256,1024]{1,0:T(8,128)} %copy-done.17, f32[864,256]{1,0:T(8,128)} %copy-done.24, f32[864,256]{1,0:T(8,128)} %collective-permute-done.69.refs_4_, f32[256,1024]{1,0:T(8,128)} %copy-done.17, f32[9056]{0:T(1024)} %copy-done.60, ...), custom_call_target="tpu_custom_call" | custom-call | flops 1 | bytes 1 | tf_op jit(solution)/shard_map/joined/pallas_call | solution.py:130
  (320 shorter events, 116.5 us)
Async XLA Ops:
  2.9 23.9 %collective-permute-start.3 = (f32[256,512]{1,0:T(8,128)S(1)}, f32[256,512]{1,0:T(8,128)S(1)}, u32[]{:S(2)}, u32[]{:S(2)}) collective-permute-start(f32[256,512]{1,0:T(8,128)S(1)} %dynamic-slice_convert_fusion.1), channel_id=1, source_target_pairs={{0,8},{1,9},{2,10},{3,11},{4,12},{5,13},{6,14},{7,15},{8,0},{9,1},... | collective-permute-start | bytes 1572872 | tf_op jit(solution)/shard_map/ppermute | solution.py:532
  31.2 25.3 %collective-permute-start.7 = (f32[256,1024]{1,0:T(8,128)S(1)}, f32[256,1024]{1,0:T(8,128)S(1)}, u32[]{:S(2)}, u32[]{:S(2)}) collective-permute-start(f32[256,1024]{1,0:T(8,128)S(1)} %add.94), channel_id=1, source_target_pairs={{0,2},{1,3},{2,0},{3,1},{4,6},{5,7},{6,4},{7,5},{8,10},{9,11},{10,... | collective-permute-start | bytes 3145736 | tf_op jit(solution)/shard_map/ppermute | solution.py:532
  32.8 24.0 %collective-permute-start.9 = (f32[128,1024]{1,0:T(8,128)S(1)}, f32[128,1024]{1,0:T(8,128)S(1)}, u32[]{:S(2)}, u32[]{:S(2)}) collective-permute-start(f32[128,1024]{1,0:T(8,128)S(1)} %get-tuple-element.167), channel_id=1, source_target_pairs={{0,4},{1,5},{2,6},{3,7},{4,0},{5,1},{6,2},{7,3},{8,12},{9,13},{10,... | collective-permute-start | bytes 1572872 | tf_op jit(solution)/shard_map/ppermute | solution.py:532
  34.3 25.6 %collective-permute-start.10 = (f32[128,1024]{1,0:T(8,128)S(1)}, f32[128,1024]{1,0:T(8,128)}, u32[]{:S(2)}, u32[]{:S(2)}) collective-permute-start(f32[128,1024]{1,0:T(8,128)S(1)} %get-tuple-element.168), channel_id=1, source_target_pairs={{0,16},{1,17},{2,18},{3,19},{4,20},{5,21},{6,22},{7,23},{8,24},{9,... | collective-permute-start | bytes 1572872 | tf_op jit(solution)/shard_map/ppermute | solution.py:532
  84.8 25.3 %collective-permute-start.22 = (f32[256,1024]{1,0:T(8,128)S(1)}, f32[256,1024]{1,0:T(8,128)S(1)}, u32[]{:S(2)}, u32[]{:S(2)}) collective-permute-start(f32[256,1024]{1,0:T(8,128)S(1)} %add.99), channel_id=1, source_target_pairs={{0,2},{1,3},{2,0},{3,1},{4,6},{5,7},{6,4},{7,5},{8,10},{9,11},{10,... | collective-permute-start | bytes 3145736 | tf_op jit(solution)/shard_map/ppermute | solution.py:532
  85.6 24.7 %collective-permute-start.21 = (f32[256,1024]{1,0:T(8,128)S(1)}, f32[256,1024]{1,0:T(8,128)S(1)}, u32[]{:S(2)}, u32[]{:S(2)}) collective-permute-start(f32[256,1024]{1,0:T(8,128)S(1)} %copy-done.65), channel_id=1, source_target_pairs={{0,1},{1,0},{2,3},{3,2},{4,5},{5,4},{6,7},{7,6},{8,9},{9,8},{10,11... | collective-permute-start | bytes 3145736 | tf_op jit(solution)/shard_map/ppermute | solution.py:532
  85.8 26.6 %collective-permute-start.24 = (f32[256,512]{1,0:T(8,128)S(1)}, f32[256,512]{1,0:T(8,128)}, u32[]{:S(2)}, u32[]{:S(2)}) collective-permute-start(f32[256,512]{1,0:T(8,128)S(1)} %constant_dynamic-slice_fusion), channel_id=1, source_target_pairs={{0,16},{1,17},{2,18},{3,19},{4,20},{5,21},{6,22},{7,23},{8,24},{9,... | collective-permute-start | bytes 1572872 | tf_op jit(solution)/shard_map/ppermute | solution.py:532
  88.1 24.3 %collective-permute-start.23 = (f32[256,512]{1,0:T(8,128)S(1)}, f32[256,512]{1,0:T(8,128)S(1)}, u32[]{:S(2)}, u32[]{:S(2)}) collective-permute-start(f32[256,512]{1,0:T(8,128)S(1)} %constant_dynamic-slice_fusion), channel_id=1, source_target_pairs={{0,8},{1,9},{2,10},{3,11},{4,12},{5,13},{6,14},{7,15},{8,0},{9,1},... | collective-permute-start | bytes 1572872 | tf_op jit(solution)/shard_map/ppermute | solution.py:532
  88.4 24.0 %collective-permute-start.25 = (f32[128,1024]{1,0:T(8,128)S(1)}, f32[128,1024]{1,0:T(8,128)}, u32[]{:S(2)}, u32[]{:S(2)}) collective-permute-start(f32[128,1024]{1,0:T(8,128)S(1)} %pad_maximum_fusion), channel_id=1, source_target_pairs={{0,4},{1,5},{2,6},{3,7},{4,0},{5,1},{6,2},{7,3},{8,12},{9,13},{10,... | collective-permute-start | bytes 1572872 | tf_op jit(solution)/shard_map/ppermute | solution.py:532
  125.2 29.2 %collective-permute-start.32 = (f32[256,1024]{1,0:T(8,128)}, f32[256,1024]{1,0:T(8,128)S(1)}, u32[]{:S(2)}, u32[]{:S(2)}) collective-permute-start(f32[256,1024]{1,0:T(8,128)} %get-tuple-element.201), channel_id=1, source_target_pairs={{0,4},{1,5},{2,6},{3,7},{4,0},{5,1},{6,2},{7,3},{8,12},{9,13},{10,... | collective-permute-start | bytes 3145736 | tf_op jit(solution)/shard_map/ppermute | solution.py:532
  126.8 26.2 %collective-permute-start.34 = (f32[256,512]{1,0:T(8,128)}, f32[256,512]{1,0:T(8,128)S(1)}, u32[]{:S(2)}, u32[]{:S(2)}) collective-permute-start(f32[256,512]{1,0:T(8,128)} %copy-done.55), channel_id=1, source_target_pairs={{0,2},{1,3},{2,0},{3,1},{4,6},{5,7},{6,4},{7,5},{8,10},{9,11},{10,... | collective-permute-start | bytes 1572872 | tf_op jit(solution)/shard_map/ppermute | solution.py:532
  127.3 25.7 %collective-permute-start.35 = (f32[256,512]{1,0:T(8,128)}, f32[256,512]{1,0:T(8,128)S(1)}, u32[]{:S(2)}, u32[]{:S(2)}) collective-permute-start(f32[256,512]{1,0:T(8,128)} %collective-permute-done.24.refs_3_), channel_id=1, source_target_pairs={{0,2},{1,3},{2,0},{3,1},{4,6},{5,7},{6,4},{7,5},{8,10},{9,11},{10,... | collective-permute-start | bytes 1572872 | tf_op jit(solution)/shard_map/ppermute | solution.py:532
  128.8 25.6 %collective-permute-start.33 = (f32[256,512]{1,0:T(8,128)}, f32[256,512]{1,0:T(8,128)}, u32[]{:S(2)}, u32[]{:S(2)}) collective-permute-start(f32[256,512]{1,0:T(8,128)} %get-tuple-element.203), channel_id=1, source_target_pairs={{0,16},{1,17},{2,18},{3,19},{4,20},{5,21},{6,22},{7,23},{8,24},{9,... | collective-permute-start | bytes 1572872 | tf_op jit(solution)/shard_map/ppermute | solution.py:532
  198.8 24.5 %collective-permute-start.54 = (f32[256,512]{1,0:T(8,128)}, f32[256,512]{1,0:T(8,128)S(1)}, u32[]{:S(2)}, u32[]{:S(2)}) collective-permute-start(f32[256,512]{1,0:T(8,128)} %constant_dynamic-update-slice_fusion.refs_15_), channel_id=1, source_target_pairs={{0,1},{1,0},{2,3},{3,2},{4,5},{5,4},{6,7},{7,6},{8,9},{9,8},{10,11... | collective-permute-start | bytes 1572872 | tf_op jit(solution)/shard_map/ppermute | solution.py:532
  198.9 24.4 %collective-permute-start.53 = (f32[256,512]{1,0:T(8,128)}, f32[256,512]{1,0:T(8,128)}, u32[]{:S(2)}, u32[]{:S(2)}) collective-permute-start(f32[256,512]{1,0:T(8,128)} %constant_dynamic-update-slice_fusion.refs_15_), channel_id=1, source_target_pairs={{0,2},{1,3},{2,0},{3,1},{4,6},{5,7},{6,4},{7,5},{8,10},{9,11},{10,... | collective-permute-start | bytes 1572872 | tf_op jit(solution)/shard_map/ppermute | solution.py:532
  199.6 23.6 %collective-permute-start.51 = (f32[256,512]{1,0:T(8,128)}, f32[256,512]{1,0:T(8,128)}, u32[]{:S(2)}, u32[]{:S(2)}) collective-permute-start(f32[256,512]{1,0:T(8,128)} %constant_dynamic-update-slice_fusion.refs_15_), channel_id=1, source_target_pairs={{0,8},{1,9},{2,10},{3,11},{4,12},{5,13},{6,14},{7,15},{8,0},{9,1},... | collective-permute-start | bytes 1572872 | tf_op jit(solution)/shard_map/ppermute | solution.py:532
  199.6 25.0 %collective-permute-start.52 = (f32[256,512]{1,0:T(8,128)}, f32[256,512]{1,0:T(8,128)}, u32[]{:S(2)}, u32[]{:S(2)}) collective-permute-start(f32[256,512]{1,0:T(8,128)} %copy-done.29), channel_id=1, source_target_pairs={{0,2},{1,3},{2,0},{3,1},{4,6},{5,7},{6,4},{7,5},{8,10},{9,11},{10,... | collective-permute-start | bytes 1572872 | tf_op jit(solution)/shard_map/ppermute | solution.py:532
  241.8 26.3 %collective-permute-start.62 = (f32[256,1024]{1,0:T(8,128)}, f32[256,1024]{1,0:T(8,128)S(1)}, u32[]{:S(2)}, u32[]{:S(2)}) collective-permute-start(f32[256,1024]{1,0:T(8,128)} %add.101), channel_id=1, source_target_pairs={{0,2},{1,3},{2,0},{3,1},{4,6},{5,7},{6,4},{7,5},{8,10},{9,11},{10,... | collective-permute-start | bytes 3145736 | tf_op jit(solution)/shard_map/ppermute | solution.py:532
  243.1 25.0 %collective-permute-start.61 = (f32[864,256]{1,0:T(8,128)}, f32[864,256]{1,0:T(8,128)S(1)}, u32[]{:S(2)}, u32[]{:S(2)}) collective-permute-start(f32[864,256]{1,0:T(8,128)} %get-tuple-element.253), channel_id=1, source_target_pairs={{0,8},{1,9},{2,10},{3,11},{4,12},{5,13},{6,14},{7,15},{8,0},{9,1},... | collective-permute-start | bytes 2654216 | tf_op jit(solution)/shard_map/ppermute | solution.py:532
  268.1 25.0 %collective-permute-start.63 = (f32[256,1024]{1,0:T(8,128)}, f32[256,1024]{1,0:T(8,128)}, u32[]{:S(2)}, u32[]{:S(2)}) collective-permute-start(f32[256,1024]{1,0:T(8,128)} %add.97), channel_id=1, source_target_pairs={{0,2},{1,3},{2,0},{3,1},{4,6},{5,7},{6,4},{7,5},{8,10},{9,11},{10,... | collective-permute-start | bytes 3145736 | tf_op jit(solution)/shard_map/ppermute | solution.py:532
  271.4 23.6 %collective-permute-start.66 = (f32[256,1024]{1,0:T(8,128)}, f32[256,1024]{1,0:T(8,128)}, u32[]{:S(2)}, u32[]{:S(2)}) collective-permute-start(f32[256,1024]{1,0:T(8,128)} %add.104.refs_4_), channel_id=1, source_target_pairs={{0,1},{1,0},{2,3},{3,2},{4,5},{5,4},{6,7},{7,6},{8,9},{9,8},{10,11... | collective-permute-start | bytes 3145736 | tf_op jit(solution)/shard_map/ppermute | solution.py:532
  271.4 23.6 %collective-permute-start.64 = (f32[864,256]{1,0:T(8,128)S(1)}, f32[864,256]{1,0:T(8,128)}, u32[]{:S(2)}, u32[]{:S(2)}) collective-permute-start(f32[864,256]{1,0:T(8,128)S(1)} %copy-done.66), channel_id=1, source_target_pairs={{0,8},{1,9},{2,10},{3,11},{4,12},{5,13},{6,14},{7,15},{8,0},{9,1},... | collective-permute-start | bytes 2654216 | tf_op jit(solution)/shard_map/ppermute | solution.py:532
  295.0 24.2 %collective-permute-start.67 = (f32[256,1024]{1,0:T(8,128)S(1)}, f32[256,1024]{1,0:T(8,128)S(1)}, u32[]{:S(2)}, u32[]{:S(2)}) collective-permute-start(f32[256,1024]{1,0:T(8,128)S(1)} %add_add_fusion.refs_1_), channel_id=1, source_target_pairs={{0,1},{1,0},{2,3},{3,2},{4,5},{5,4},{6,7},{7,6},{8,9},{9,8},{10,11... | collective-permute-start | bytes 3145736 | tf_op jit(solution)/shard_map/ppermute | solution.py:532
  295.0 24.1 %collective-permute-start.68 = (f32[864,256]{1,0:T(8,128)}, f32[864,256]{1,0:T(8,128)S(1)}, u32[]{:S(2)}, u32[]{:S(2)}) collective-permute-start(f32[864,256]{1,0:T(8,128)} %get-tuple-element.280), channel_id=1, source_target_pairs={{0,8},{1,9},{2,10},{3,11},{4,12},{5,13},{6,14},{7,15},{8,0},{9,1},... | collective-permute-start | bytes 2654216 | tf_op jit(solution)/shard_map/ppermute | solution.py:532
  (119 other events, 1088.2 us)
